TPU v7x, 32 devices: a whole 2x2x4 slice. The times are simulated.
32 devices in a mesh: dp: 2 (over x), row: 4 (over z), col: 4 (over y, core).
Axes of the slice: x: 2, y: 2, z: 4, core: 2. Of those that a mesh axis runs over, the one named last changes fastest.
Arguments:
- tokens: bfloat16 [4, 2048, 2048], P('dp', 'row', 'col'), may hold values from -6 to 6
- lengths: int32 [4], P('dp'), may hold values from 682 to 2048, as said below
- cotangent: bfloat16 [4, 2048, 2048], P('dp', 'row', 'col'), may hold values from -6 to 6
- norm1_gain: float32 [2048], P('col'), may hold values from 0.25 to 1.75
- norm1_bias: float32 [2048], P('col'), may hold values from -3 to 3
- query_weight: bfloat16 [2048, 2048], P('col', 'row'), may hold values from -0.125 to 0.125
- kv_weight: bfloat16 [2048, 256], P('col'), may hold values from -0.125 to 0.125
- out_weight: bfloat16 [2048, 2048], P('row', 'col'), may hold values from -1 to 1
- norm2_gain: float32 [2048], P('col'), may hold values from 0.25 to 1.75
- norm2_bias: float32 [2048], P('col'), may hold values from -3 to 3
- up_weight: bfloat16 [2048, 8192], P('col', 'row'), may hold values from -0.125 to 0.125
- down_weight: bfloat16 [8192, 2048], P('row', 'col'), may hold values from -0.0625 to 0.0625
Outputs:
- out: bfloat16 [4, 2048, 2048], P('dp', 'row', 'col')
- grad_input: bfloat16 [4, 2048, 2048], P('dp', 'row', 'col')
- grad_norm1_gain: float32 [2048], P('col')
- grad_norm1_bias: float32 [2048], P('col')
- grad_query_weight: float32 [2048, 2048], P('col', 'row')
- grad_kv_weight: float32 [2048, 256], P('col')
- grad_out_weight: float32 [2048, 2048], P('row', 'col')
- grad_norm2_gain: float32 [2048], P('col')
- grad_norm2_bias: float32 [2048], P('col')
- grad_up_weight: float32 [2048, 8192], P('col', 'row')
- grad_down_weight: float32 [8192, 2048], P('row', 'col')
Inputs may be any that keep to these rules, and one draw needn't show every extreme that they name: `lengths`: entry s is the number of valid slots of sequence s; sequences s * 2 to s * 2 + 1 belong to index s of dp. Some sequence has all 2048 slots valid.
All inputs are finite; a program needn't handle non-finite values.
Results may differ from a plain program's by a relative error of at most 0.02.
Values may be sent and summed in bfloat16 or wider, within the bound.
A program may use at most 256 MiB of HBM per device.

v0:
```python
import jax
import jax.numpy as jnp
from jax import lax
from jax.sharding import PartitionSpec as P

eps = 1e-05
BF = jnp.bfloat16
F32 = jnp.float32


def mm(a, b, ca, cb):
    return lax.dot_general(a, b, (((ca,), (cb,)), ((), ())), preferred_element_type=F32)


def norm_stats(hidden):
    centre = jnp.mean(hidden, axis=1, keepdims=True)
    spread = jnp.mean(hidden * hidden, axis=1, keepdims=True) - centre * centre
    return (centre, lax.rsqrt(spread + eps))


def norm_apply(hidden, centre, inverse, gain, bias, keep):
    return (keep * ((hidden - centre) * inverse * gain + bias)).astype(BF)


def norm_backward(gradient, normed, inverse, gain, keep):
    masked = keep * gradient
    scaled = masked * gain
    first = jnp.mean(scaled, axis=1, keepdims=True)
    second = jnp.mean(scaled * normed, axis=1, keepdims=True)
    result = inverse * (scaled - first - normed * second)
    return (result, jnp.sum(masked * normed, axis=0), jnp.sum(masked, axis=0))


def turn(weight):
    return lax.all_to_all(weight, "col", 0, 1, tiled=True)


def turn_back(rows):
    return lax.all_to_all(rows, "col", 1, 0, tiled=True)


def gather(x, axes, dim=0):
    return lax.all_gather(x, axes, axis=dim, tiled=True)


def scatter(x, axes):
    return lax.psum_scatter(x, axes, scatter_dimension=0, tiled=True)


def pairs_allowed(first, count, keys, length):
    q = first + jnp.arange(count, dtype=jnp.int32)[:, None]
    k = jnp.arange(keys, dtype=jnp.int32)[None, :]
    return (k <= q) & (k < length)


def attend(queries, kv, lengths, first):
    b, t, width = queries.shape
    hd = kv.shape[2] // 2
    outs, logs = ([], [])
    for s in range(b):
        keys, values = (kv[s, :, :hd], kv[s, :, hd:])
        allowed = pairs_allowed(first, t, kv.shape[1], lengths[s])
        for h in range(width // hd):
            q = queries[s, :, h * hd : (h + 1) * hd]
            scores = jnp.where(allowed, mm(q, keys, 1, 1) * hd ** (-0.5), -jnp.inf)
            top = jnp.max(scores, axis=1, keepdims=True)
            log_total = top + jnp.log(jnp.sum(jnp.exp(scores - top), axis=1, keepdims=True))
            weights = jnp.exp(scores - log_total).astype(BF)
            outs.append(mm(weights, values, 1, 0).astype(BF))
            logs.append(log_total)
    n = width // hd
    out = jnp.stack([jnp.concatenate(outs[s * n : (s + 1) * n], axis=1) for s in range(b)])
    log = jnp.stack([jnp.concatenate(logs[s * n : (s + 1) * n], axis=1) for s in range(b)])
    return (out, log)


def attend_back(queries, kv, lengths, first, logs, grad):
    b, t, width = queries.shape
    hd = kv.shape[2] // 2
    scale = hd ** (-0.5)
    dqs, dkvs = ([], [])
    for s in range(b):
        keys, values = (kv[s, :, :hd], kv[s, :, hd:])
        allowed = pairs_allowed(first, t, kv.shape[1], lengths[s])
        dk = dv = 0.0
        dq = []
        for h in range(width // hd):
            q = queries[s, :, h * hd : (h + 1) * hd]
            g = grad[s, :, h * hd : (h + 1) * hd]
            scores = jnp.where(allowed, mm(q, keys, 1, 1) * scale, -jnp.inf)
            p = jnp.exp(scores - logs[s, :, h : h + 1])
            dp = mm(g, values, 1, 1)
            ds = (p * (dp - jnp.sum(p * dp, axis=1, keepdims=True))).astype(BF)
            dq.append((mm(ds, keys, 1, 0) * scale).astype(BF))
            dk = dk + mm(ds, q, 0, 0) * scale
            dv = dv + mm(p.astype(BF), g, 0, 0)
        dqs.append(jnp.concatenate(dq, axis=1))
        dkvs.append(jnp.concatenate([dk, dv], axis=1).astype(BF))
    return (jnp.stack(dqs), jnp.stack(dkvs))


def local(
    tokens,
    lengths,
    cotangent,
    norm1_gain,
    norm1_bias,
    query_weight,
    kv_weight,
    out_weight,
    norm2_gain,
    norm2_bias,
    up_weight,
    down_weight,
):
    b, t, f = tokens.shape
    nd, nr, nc = (lax.axis_size(a) for a in ("dp", "row", "col"))
    dp, row, col = (lax.axis_index(a) for a in ("dp", "row", "col"))
    m, d = (b * t, f * nc)
    own = m // nc
    hd = kv_weight.shape[1] // 2
    plane = ("dp", "col")
    slot = row * t + jnp.arange(t, dtype=jnp.int32)
    keep = (slot[None, :] < lengths[:, None]).astype(F32).reshape(m, 1)

    def mine(x):
        return lax.dynamic_slice_in_dim(x, col * own, own, 0)

    def half(w):
        n = w.shape[0] // nd
        return lax.dynamic_slice_in_dim(w, dp * n, n, 0)

    wq = gather(turn(query_weight.T), "row")
    wo = gather(turn(out_weight), "row")
    wu = gather(turn(half(up_weight.T)), "row")
    wd = gather(turn(half(down_weight)), "row")
    wkv = gather(kv_weight, "col")
    vectors = gather(jnp.stack([norm1_gain, norm1_bias, norm2_gain, norm2_bias]), "col", 1)
    gain1, bias1, gain2, bias2 = (vectors[i : i + 1] for i in range(4))
    x = gather(tokens.reshape(m, f), "col", 1)
    grad_final = (keep * cotangent.reshape(m, f).astype(F32)).astype(BF)
    grad_own = turn(grad_final)
    grad_all = gather(grad_own, plane)
    keep_own = mine(keep)
    centre, inverse = norm_stats(x.astype(F32))
    one = norm_apply(x.astype(F32), centre, inverse, gain1, bias1, keep)
    one_own = mine(one)
    queries = mm(one, wq, 1, 1).astype(BF).reshape(b, t, -1)
    kv_own = mm(one_own, wkv, 1, 0).astype(BF)
    kv = gather(kv_own, ("row", "col")).reshape(nr, b, t, 2 * hd)
    kv = kv.transpose(1, 0, 2, 3).reshape(b, nr * t, 2 * hd)
    attended, logs = attend(queries, kv, lengths, row * t)
    attended = attended.reshape(m, -1)
    x_own = mine(x).astype(F32)
    middle = x_own + scatter(mm(attended, wo, 1, 0).astype(BF), "col").astype(F32)
    centre2, inverse2 = norm_stats(middle)
    two_own = norm_apply(middle, centre2, inverse2, gain2, bias2, keep_own)
    two = gather(two_own, plane)
    sums = mm(two, wu, 1, 1)
    activated, pull = jax.vjp(lambda v: jax.nn.gelu(v, approximate=True), sums)
    activated = activated.astype(BF)
    ffn = scatter(mm(activated, wd, 1, 0).astype(BF), plane)
    out = turn_back((keep_own * (middle + ffn.astype(F32))).astype(BF))
    grad_act = mm(grad_all, wd, 1, 1)
    grad_up = pull(grad_act)[0].astype(BF)
    d_down = scatter(mm(activated, grad_all, 0, 0).astype(BF), "row")
    d_up = scatter(mm(grad_up, two, 0, 0).astype(BF), "row")
    e_two = scatter(mm(grad_up, wu, 1, 0).astype(BF), plane).astype(F32)
    normed2 = (middle - centre2) * inverse2
    back_two, g_gain2, g_bias2 = norm_backward(e_two, normed2, inverse2, gain2, keep_own)
    grad_middle = grad_own.astype(F32) + back_two
    grad_attn = gather(grad_middle.astype(BF), "col")
    grad_att = mm(grad_attn, wo, 1, 1).astype(BF)
    d_out = scatter(mm(attended, grad_attn, 0, 0).astype(BF), "row")
    dq, dkv = attend_back(queries, kv, lengths, row * t, logs, grad_att.reshape(b, t, -1))
    dq = dq.reshape(m, -1)
    dkv = dkv.reshape(b, nr, t, 2 * hd).transpose(1, 0, 2, 3).reshape(nr * m, 2 * hd)
    dkv_own = scatter(dkv, ("row", "col"))
    d_query = scatter(mm(dq, one, 0, 0).astype(BF), "row")
    e_one = scatter(mm(dq, wq, 1, 0).astype(BF), "col").astype(F32) + mm(dkv_own, wkv, 1, 1)
    normed1 = (x_own - mine(centre)) * mine(inverse)
    back_one, g_gain1, g_bias1 = norm_backward(e_one, normed1, mine(inverse), gain1, keep_own)
    grad_in = turn_back((grad_middle + back_one).astype(BF))
    d_kv = scatter(mm(one_own, dkv_own, 0, 0).astype(BF), "col")
    d_kv = lax.psum(d_kv, ("dp", "row")).astype(F32)
    small = lax.psum(jnp.stack([g_gain1, g_bias1, g_gain2, g_bias2]), ("dp", "row", "col"))
    small = lax.dynamic_slice_in_dim(small, col * f, f, 1)
    d_query = lax.psum(turn_back(d_query), "dp").astype(F32).T
    d_out = lax.psum(turn_back(d_out), "dp").astype(F32)
    d_up = gather(turn_back(d_up), "dp").astype(F32).T
    d_down = gather(turn_back(d_down), "dp").astype(F32)
    return (
        out.reshape(b, t, f),
        grad_in.reshape(b, t, f),
        small[0],
        small[1],
        d_query,
        d_kv,
        d_out,
        small[2],
        small[3],
        d_up,
        d_down,
    )


def solution(mesh):
    act, vec = (P("dp", "row", "col"), P("col"))
    wide, tall = (P("col", "row"), P("row", "col"))
    return jax.shard_map(
        local,
        mesh=mesh,
        in_specs=(act, P("dp"), act, vec, vec, wide, P("col", None), tall, vec, vec, wide, tall),
        out_specs=(act, act, vec, vec, wide, P("col", None), tall, vec, vec, wide, tall),
        check_vma=False,
    )
```

profile of v0, /device:TPU:0, one launch (start us, length us, event | category | flops | bytes accessed | tf_op | source)
XLA Modules:
  0.0 1477.3 jit_solution(9713727474657189356)
XLA Ops:
  82.3 31.9 %all-gather.15.cloned.1.call-done = bf16[512,2048]{0,1:T(8,128)(2,1)} async-done(((bf16[128,2048]{0,1:T(8,128)(2,1)}), bf16[512,2048]{0,1:T(8,128)(2,1)}) %all-gather.15.cloned.1.call-update) | async-done | bytes 2097168 | tf_op jit(solution)/shard_map/all_gather | solution.py:43
  119.4 37.1 %all-gather.19.cloned.1.call-done = bf16[4096,256]{1,0:T(8,128)(2,1)} async-done(((bf16[256,256]{1,0:T(8,128)(2,1)}), bf16[4096,256]{1,0:T(8,128)(2,1)}) %all-gather.19.cloned.1.call-update) | async-done | bytes 2097168 | tf_op jit(solution)/shard_map/all_gather | solution.py:43
  184.7 18.8 %all-gather.21.cloned.1.call-done = bf16[512,2048]{0,1:T(8,128)(2,1)} async-done(((bf16[128,2048]{0,1:T(8,128)(2,1)}), bf16[512,2048]{0,1:T(8,128)(2,1)}) %all-gather.21.cloned.1.call-update) | async-done | bytes 2097168 | tf_op jit(solution)/shard_map/all_gather | solution.py:43
  229.1 28.4 %all_to_all.202 = bf16[4,256,512]{2,1,0:T(8,128)(2,1)S(1)} all-to-all(bf16[4,256,512]{2,1,0:T(8,128)(2,1)S(1)} %fusion.58), channel_id=1, replica_groups=mesh['dp'=2,'row'=4,'col'=4] {'col'}, dimensions={0} | all-to-all | bytes 2097152 | tf_op jit(solution)/shard_map/all_to_all | solution.py:35
  284.8 62.0 %all-gather.27.cloned.1.call-done = bf16[1024,2048]{0,1:T(8,128)(2,1)} async-done(((bf16[256,2048]{0,1:T(8,128)(2,1)}), bf16[1024,2048]{0,1:T(8,128)(2,1)}) %all-gather.27.cloned.1.call-update) | async-done | bytes 4194320 | tf_op jit(solution)/shard_map/all_gather | solution.py:43
  346.8 55.2 %all-gather.29.cloned.1.call-done = bf16[2048,2048]{1,0:T(8,128)(2,1)} async-done(((bf16[256,2048]{1,0:T(8,128)(2,1)}), bf16[2048,2048]{1,0:T(8,128)(2,1)}) %all-gather.29.cloned.1.call-update) | async-done | bytes 8388624 | tf_op jit(solution)/shard_map/all_gather | solution.py:43
  416.4 67.8 %all-gather.25.cloned.1.call-done = bf16[1024,2048]{0,1:T(8,128)(2,1)} async-done(((bf16[256,2048]{0,1:T(8,128)(2,1)}), bf16[1024,2048]{0,1:T(8,128)(2,1)}) %all-gather.25.cloned.1.call-update) | async-done | bytes 4194320 | tf_op jit(solution)/shard_map/all_gather | solution.py:43
  484.2 55.1 %all-gather.23.cloned.1.call-done = bf16[2048,2048]{1,0:T(8,128)(2,1)} async-done(((bf16[256,2048]{1,0:T(8,128)(2,1)}), bf16[2048,2048]{1,0:T(8,128)(2,1)}) %all-gather.23.cloned.1.call-update) | async-done | bytes 8388624 | tf_op jit(solution)/shard_map/all_gather | solution.py:43
  539.3 22.2 %fusion.6 = (bf16[2048,1024]{1,0:T(8,128)(2,1)S(1)}, f32[2048,1024]{1,0:T(8,128)}) fusion(f32[2048,1024]{1,0:T(8,128)} %fusion.125, bf16[2048,2048]{1,0:T(8,128)(2,1)} %all-gather.23.cloned.1.call-done, bf16[1024,2048]{0,1:T(8,128)(2,1)} %all-gather.25.cloned.1.call-done), kind=kOutput, calls=%fused_computation.11 | convolution fusion | flops 8631877632 | bytes 33554432 | tf_op jit(solution)/shard_map/dot_general | solution.py:12
  590.0 55.9 %reduce-scatter.15.cloned.1.call-done = bf16[256,2048]{1,0:T(8,128)(2,1)} async-done(((bf16[2048,2048]{1,0:T(8,128)(2,1)}), bf16[256,2048]{1,0:T(8,128)(2,1)}) %reduce-scatter.15.cloned.1.call-update) | async-done | bytes 1048592 | tf_op jit(solution)/shard_map/reduce_scatter | solution.py:47
  648.7 71.8 %reduce-scatter.13.cloned.1.call-done = bf16[256,2048]{1,0:T(8,128)(2,1)} async-done(((bf16[2048,2048]{1,0:T(8,128)(2,1)}), bf16[256,2048]{1,0:T(8,128)(2,1)}) %reduce-scatter.13.cloned.1.call-update) | async-done | bytes 1048592 | tf_op jit(solution)/shard_map/reduce_scatter | solution.py:47
  725.9 34.5 %all-gather.31.cloned.1.call-done = bf16[1024,2048]{1,0:T(8,128)(2,1)} async-done(((bf16[256,2048]{1,0:T(8,128)(2,1)}), bf16[1024,2048]{1,0:T(8,128)(2,1)}) %all-gather.31.cloned.1.call-update) | async-done | bytes 4194320 | tf_op jit(solution)/shard_map/all_gather | solution.py:43
  913.4 75.8 %reduce-scatter.29.cloned.1.call-done = bf16[256,2048]{1,0:T(8,128)(2,1)} async-done(((bf16[1024,2048]{1,0:T(8,128)(2,1)}), bf16[256,2048]{1,0:T(8,128)(2,1)}) %reduce-scatter.29.cloned.1.call-update) | async-done | bytes 1048592 | tf_op jit(solution)/shard_map/reduce_scatter | solution.py:47
  990.5 17.6 %all_to_all.204 = bf16[256,4,512]{2,0,1:T(8,128)(2,1)} all-to-all(bf16[256,4,512]{2,0,1:T(8,128)(2,1)S(1)} %bitcast.415), channel_id=1, replica_groups=mesh['dp'=2,'row'=4,'col'=4] {'col'}, dimensions={1} | all-to-all | bytes 2097152 | tf_op jit(solution)/shard_map/all_to_all | solution.py:39
  1014.3 54.5 %reduce-scatter.27.cloned.1.call-done = bf16[256,2048]{1,0:T(8,128)(2,1)} async-done(((bf16[1024,2048]{1,0:T(8,128)(2,1)}), bf16[256,2048]{1,0:T(8,128)(2,1)}) %reduce-scatter.27.cloned.1.call-update) | async-done | bytes 1048592 | tf_op jit(solution)/shard_map/reduce_scatter | solution.py:47
  1088.5 26.9 %reduce-scatter.21.cloned.1.call-done = bf16[128,2048]{1,0:T(8,128)(2,1)} async-done(((bf16[512,2048]{1,0:T(8,128)(2,1)}), bf16[128,2048]{1,0:T(8,128)(2,1)}) %reduce-scatter.21.cloned.1.call-update) | async-done | bytes 524304 | tf_op jit(solution)/shard_map/reduce_scatter | solution.py:47
  1120.7 40.1 %reduce-scatter.25.cloned.1.call-done = bf16[128,2048]{1,0:T(8,128)(2,1)} async-done(((bf16[512,2048]{1,0:T(8,128)(2,1)}), bf16[128,2048]{1,0:T(8,128)(2,1)}) %reduce-scatter.25.cloned.1.call-update) | async-done | bytes 524304 | tf_op jit(solution)/shard_map/reduce_scatter | solution.py:47
  1166.3 21.8 %reduce-scatter.23.cloned.1.call-done = bf16[512,256]{1,0:T(8,128)(2,1)} async-done(((bf16[2048,256]{1,0:T(8,128)(2,1)}), bf16[512,256]{1,0:T(8,128)(2,1)}) %reduce-scatter.23.cloned.1.call-update) | async-done | bytes 262160 | tf_op jit(solution)/shard_map/reduce_scatter | solution.py:47
  1189.6 33.1 %all-gather.35.cloned.1.call-done = bf16[2048,512]{1,0:T(8,128)(2,1)} async-done(((bf16[1024,512]{1,0:T(8,128)(2,1)}), bf16[2048,512]{1,0:T(8,128)(2,1)}) %all-gather.35.cloned.1.call-update) | async-done | bytes 2097168 | tf_op jit(solution)/shard_map/all_gather | solution.py:43
  1233.2 37.7 %reduce-scatter.17.cloned.1.call-done = bf16[256,2048]{1,0:T(8,128)(2,1)} async-done(((bf16[1024,2048]{1,0:T(8,128)(2,1)}), bf16[256,2048]{1,0:T(8,128)(2,1)}) %reduce-scatter.17.cloned.1.call-update) | async-done | bytes 1048592 | tf_op jit(solution)/shard_map/reduce_scatter | solution.py:47
  1281.4 24.4 %all-gather.33.cloned.1.call-done = bf16[2048,512]{0,1:T(8,128)(2,1)} async-done(((bf16[1024,512]{0,1:T(8,128)(2,1)}), bf16[2048,512]{0,1:T(8,128)(2,1)}) %all-gather.33.cloned.1.call-update) | async-done | bytes 2097168 | tf_op jit(solution)/shard_map/all_gather | solution.py:43
  1310.1 69.8 %all-reduce.4.cloned.1.call-done = bf16[512,256]{1,0:T(8,128)(2,1)} async-done(((bf16[512,256]{1,0:T(8,128)(2,1)}), bf16[512,256]{1,0:T(8,128)(2,1)}) %all-reduce.4.cloned.1.call-update) | async-done | bytes 262160 | tf_op jit(solution)/shard_map/psum | solution.py:185
  1381.6 40.7 %all-reduce.6.cloned.1.call-done = (bf16[512,512]{1,0:T(8,128)(2,1)}, bf16[512,512]{1,0:T(8,128)(2,1)}) async-done(((bf16[512,512]{1,0:T(8,128)(2,1)}, bf16[512,512]{1,0:T(8,128)(2,1)}), (bf16[512,512]{1,0:T(8,128)(2,1)}, bf16[512,512]{1,0:T(8,128)(2,1)})) %all-reduce.6.cloned.1.call-update) | async-done | bytes 1048592 | tf_op jit(solution)/shard_map/psum | solution.py:188
  1426.6 39.5 %psum.28 = f32[4,2048]{1,0:T(4,128)S(1)} all-reduce(f32[4,2048]{1,0:T(4,128)S(1)} %pad_maximum_fusion.2), channel_id=1, replica_groups=mesh['dp'=2,'row'=4,'col'=4] {'dp','row','col'}, use_global_device_ids=true, to_apply=%region_41.42 | all-reduce | flops 8192 | bytes 65536 | tf_op jit(solution)/shard_map/psum | solution.py:186
  (344 shorter events, 438.7 us)
Async XLA Ops:
  8.7 105.5 %all-gather.15.cloned.1.call-start = ((), (), s32[]{:S(2)}) async-start(), calls=%async_computation.22 | async-start | bytes 2621440 | tf_op jit(solution)/shard_map/all_gather | solution.py:43
  24.0 132.5 %all-gather.19.cloned.1.call-start = ((), (), s32[]{:S(2)}) async-start(), calls=%async_computation.24 | async-start | bytes 2228224 | tf_op jit(solution)/shard_map/all_gather | solution.py:43
  71.9 131.5 %all-gather.21.cloned.1.call-start = ((), (), s32[]{:S(2)}) async-start(), calls=%async_computation.25 | async-start | bytes 2621440 | tf_op jit(solution)/shard_map/all_gather | solution.py:43
  81.8 197.1 %reduce-scatter.11.cloned.1.call-start = ((), (), s32[]{:S(2)}) async-start(), calls=%async_computation.26 | async-start | bytes 5242880 | tf_op jit(solution)/shard_map/reduce_scatter | solution.py:47
  209.8 136.9 %all-gather.27.cloned.1.call-start = ((), (), s32[]{:S(2)}) async-start(), calls=%async_computation.29 | async-start | bytes 5242880 | tf_op jit(solution)/shard_map/all_gather | solution.py:43
  228.5 173.5 %all-gather.29.cloned.1.call-start = ((), (), s32[]{:S(2)}) async-start(), calls=%async_computation.31 | async-start | bytes 9437184 | tf_op jit(solution)/shard_map/all_gather | solution.py:43
  258.7 225.6 %all-gather.25.cloned.1.call-start = ((), (), s32[]{:S(2)}) async-start(), calls=%async_computation.28 | async-start | bytes 5242880 | tf_op jit(solution)/shard_map/all_gather | solution.py:43
  278.8 260.5 %all-gather.23.cloned.1.call-start = ((), (), s32[]{:S(2)}) async-start(), calls=%async_computation.27 | async-start | bytes 9437184 | tf_op jit(solution)/shard_map/all_gather | solution.py:43
  284.7 361.2 %reduce-scatter.15.cloned.1.call-start = ((), (), s32[]{:S(2)}) async-start(), calls=%async_computation.32 | async-start | bytes 9437184 | tf_op jit(solution)/shard_map/reduce_scatter | solution.py:47
  574.5 146.1 %reduce-scatter.13.cloned.1.call-start = ((), (), s32[]{:S(2)}) async-start(), calls=%async_computation.30 | async-start | bytes 9437184 | tf_op jit(solution)/shard_map/reduce_scatter | solution.py:47
  589.9 170.5 %all-gather.31.cloned.1.call-start = ((), (), s32[]{:S(2)}) async-start(), calls=%async_computation.33 | async-start | bytes 5242880 | tf_op jit(solution)/shard_map/all_gather | solution.py:43
  725.8 184.9 %reduce-scatter.19.cloned.1.call-start = ((), (), s32[]{:S(2)}) async-start(), calls=%async_computation.35 | async-start | bytes 2228224 | tf_op jit(solution)/shard_map/reduce_scatter | solution.py:47
  849.0 140.3 %reduce-scatter.29.cloned.1.call-start = ((), (), s32[]{:S(2)}) async-start(), calls=%async_computation.42 | async-start | bytes 5242880 | tf_op jit(solution)/shard_map/reduce_scatter | solution.py:47
  865.0 203.8 %reduce-scatter.27.cloned.1.call-start = ((), (), s32[]{:S(2)}) async-start(), calls=%async_computation.40 | async-start | bytes 5242880 | tf_op jit(solution)/shard_map/reduce_scatter | solution.py:47
  879.6 235.8 %reduce-scatter.21.cloned.1.call-start = ((), (), s32[]{:S(2)}) async-start(), calls=%async_computation.36 | async-start | bytes 2621440 | tf_op jit(solution)/shard_map/reduce_scatter | solution.py:47
  898.1 262.6 %reduce-scatter.25.cloned.1.call-start = ((), (), s32[]{:S(2)}) async-start(), calls=%async_computation.39 | async-start | bytes 2621440 | tf_op jit(solution)/shard_map/reduce_scatter | solution.py:47
  904.3 283.8 %reduce-scatter.23.cloned.1.call-start = ((), (), s32[]{:S(2)}) async-start(), calls=%async_computation.37 | async-start | bytes 1310720 | tf_op jit(solution)/shard_map/reduce_scatter | solution.py:47
  913.4 309.3 %all-gather.35.cloned.1.call-start = ((), (), s32[]{:S(2)}) async-start(), calls=%async_computation.43 | async-start | bytes 3145728 | tf_op jit(solution)/shard_map/all_gather | solution.py:43
  1008.2 262.7 %reduce-scatter.17.cloned.1.call-start = ((), (), s32[]{:S(2)}) async-start(), calls=%async_computation.34 | async-start | bytes 5242880 | tf_op jit(solution)/shard_map/reduce_scatter | solution.py:47
  1014.2 291.6 %all-gather.33.cloned.1.call-start = ((), (), s32[]{:S(2)}) async-start(), calls=%async_computation.41 | async-start | bytes 3145728 | tf_op jit(solution)/shard_map/all_gather | solution.py:43
  1162.8 66.2 %all-to-all-start.8 = ((bf16[128,4,512]{2,0,1:T(8,128)(2,1)}), bf16[128,4,512]{2,0,1:T(8,128)(2,1)S(1)}, u32[]{:S(2)}, u32[]{:S(2)}) async-start(bf16[128,4,512]{2,0,1:T(8,128)(2,1)} %bitcast.353), calls=%async_computation.16 | async-start | bytes 1048576 | tf_op jit(solution)/shard_map/all_to_all | solution.py:39
  1166.2 213.6 %all-reduce.4.cloned.1.call-start = ((), (), s32[]{:S(2)}) async-start(), calls=%async_computation.38 | async-start | bytes 524288 | tf_op jit(solution)/shard_map/psum | solution.py:185
  1232.6 189.7 %all-reduce.6.cloned.1.call-start = ((), (), s32[]{:S(2)}) async-start(), calls=%async_computation.44 | async-start | bytes 2097152 | tf_op jit(solution)/shard_map/psum | solution.py:188
  1277.1 189.7 %all-to-all-start.6 = ((bf16[256,4,512]{2,0,1:T(8,128)(2,1)}), bf16[256,4,512]{2,0,1:T(8,128)(2,1)}, u32[]{:S(2)}, u32[]{:S(2)}) async-start(bf16[256,4,512]{2,0,1:T(8,128)(2,1)} %bitcast.351), calls=%async_computation.11 | async-start | bytes 2097152 | tf_op jit(solution)/shard_map/all_to_all | solution.py:39
  (65 other events, 1431.1 us)
Sparse Core Ops, SparseCore 0:
  9.6 37.4 all-gather.12
  48.7 17.0 all-gather.16
  67.9 46.2 all-gather.14
  116.8 39.6 all-gather.18
  158.4 44.9 all-gather.20
  209.9 53.9 reduce-scatter.10
  266.2 80.5 all-gather.26
  349.4 52.5 all-gather.28
  403.6 80.5 all-gather.24
  486.7 52.5 all-gather.22
  574.6 71.3 reduce-scatter.14
  649.2 71.2 reduce-scatter.12
  725.9 34.4 all-gather.30
  849.1 61.5 reduce-scatter.18
  913.4 75.7 reduce-scatter.28
  991.5 77.2 reduce-scatter.26
  1070.9 44.3 reduce-scatter.20
  1117.6 43.1 reduce-scatter.24
  1163.9 24.1 reduce-scatter.22
  1189.6 33.1 all-gather.34
  1226.0 44.8 reduce-scatter.16
  1273.0 32.7 all-gather.32
  1309.2 70.6 all-reduce.3
  1382.7 39.5 all-reduce.5
where the time goes:
time: 1480 us
  waiting for transfers between devices  955 us (65%)
  matrix products  214 us (14%)
  blocking collectives  155 us (10%)
  other arithmetic  73.4 us (5%)
  local copies, waits for them, and re-layouts  43.2 us (3%)
  starting transfers between devices  20.2 us (1%)
  between operations  16 us (1%)
    all_gather x12, waiting for transfers between devices, gather(): return lax.all_gather(x, axes, axis=dim, tiled=True)  445 us
    reduce_scatter x10, waiting for transfers between devices, scatter(): return lax.psum_scatter(x, axes, scatter_dimension=0, tiled=True)  391 us
    dot_general x63, matrix products, mm(): lax.dot_general(a, b, (((ca,), (cb,)), ((), ())), preferred_element_type=...  214 us
    all_to_all x4, blocking collectives, turn(): return lax.all_to_all(weight, 'col', 0, 1, tiled=True)  75.5 us
    psum x1, waiting for transfers between devices, local(): d_kv = lax.psum(d_kv, ('dp', 'row')).astype(F32)  69.8 us
    psum x1, waiting for transfers between devices, local(): d_query = lax.psum(turn_back(d_query), 'dp').astype(F32).T  40.7 us
    psum x1, blocking collectives, local(): lax.psum(jnp.stack([g_gain1, g_bias1, g_gain2, g_bias2]), ('dp', 'row', '...  39.5 us
    all_to_all x2, blocking collectives, turn_back(): return lax.all_to_all(rows, 'col', 1, 0, tiled=True)  34.6 us
  transfers between devices with their start and end apart: 29, of which 24 were waited for; matrix products, arithmetic and copies ran while one was open for 13% of the time, Pallas kernels for 0%

commit v1 on v0

--- a/solution.py
+++ b/solution.py
@@ -6,6 +6,7 @@
 eps = 1e-05
 BF = jnp.bfloat16
 F32 = jnp.float32
+lift_space = lambda net_axis, body: jnp.sum(lax.all_gather(body, net_axis), axis=0)
 
 
 def mm(a, b, ca, cb):
@@ -182,7 +183,7 @@
     back_one, g_gain1, g_bias1 = norm_backward(e_one, normed1, mine(inverse), gain1, keep_own)
     grad_in = turn_back((grad_middle + back_one).astype(BF))
     d_kv = scatter(mm(one_own, dkv_own, 0, 0).astype(BF), "col")
-    d_kv = lax.psum(d_kv, ("dp", "row")).astype(F32)
+    d_kv = lift_space(("dp", "row"), d_kv).astype(F32)
     small = lax.psum(jnp.stack([g_gain1, g_bias1, g_gain2, g_bias2]), ("dp", "row", "col"))
     small = lax.dynamic_slice_in_dim(small, col * f, f, 1)
     d_query = lax.psum(turn_back(d_query), "dp").astype(F32).T

time: 1480 us -> 1420 us (0.959)
  waiting for transfers between devices: 955 us -> 889 us
    psum x1 -> x0, waiting for transfers between devices: 69.8 us -> none  [local(): d_kv = lax.psum(d_kv, ('dp', 'row')).astype(F32)]
  transfers between devices with their start and end apart: 29 -> 29, of which waited for: 24 -> 25; matrix products, arithmetic and copies ran while one was open for 13% -> 14% of each run, Pallas kernels for 0% -> 0%
where the time goes in v1:
time: 1420 us; the launch traced here: 1410 us
  waiting for transfers between devices  889 us (63%)
  matrix products  214 us (15%)
  blocking collectives  156 us (11%)
  other arithmetic  74.4 us (5%)
  local copies, waits for them, and re-layouts  43.9 us (3%)
  starting transfers between devices  20.2 us (1%)
  between operations  16 us (1%)
    all_gather x12, waiting for transfers between devices, gather(): return lax.all_gather(x, axes, axis=dim, tiled=True)  445 us
    reduce_scatter x10, waiting for transfers between devices, scatter(): return lax.psum_scatter(x, axes, scatter_dimension=0, tiled=True)  383 us
    dot_general x63, matrix products, mm(): lax.dot_general(a, b, (((ca,), (cb,)), ((), ())), preferred_element_type=...  214 us
    all_to_all x4, blocking collectives, turn(): return lax.all_to_all(weight, 'col', 0, 1, tiled=True)  75.5 us
    psum x1, blocking collectives, local(): lax.psum(jnp.stack([g_gain1, g_bias1, g_gain2, g_bias2]), ('dp', 'row', '...  40.6 us
    psum x1, waiting for transfers between devices, local(): d_query = lax.psum(turn_back(d_query), 'dp').astype(F32).T  39.1 us
    all_to_all x2, blocking collectives, turn_back(): return lax.all_to_all(rows, 'col', 1, 0, tiled=True)  34.6 us
  transfers between devices with their start and end apart: 29, of which 25 were waited for; matrix products, arithmetic and copies ran while one was open for 14% of the time, Pallas kernels for 0%

profile of v1, /device:TPU:0, one launch (start us, length us, event | category | flops | bytes accessed | tf_op | source)
XLA Modules:
  0.0 1414.2 jit_solution(1557981959748297425)
XLA Ops:
  29.6 17.6 %all-gather.15.cloned.1.call-done = bf16[1024,2048]{1,0:T(8,128)(2,1)} async-done(((bf16[1024,512]{1,0:T(8,128)(2,1)}), bf16[1024,2048]{1,0:T(8,128)(2,1)}) %all-gather.15.cloned.1.call-update) | async-done | bytes 4194320 | tf_op jit(solution)/shard_map/all_gather | solution.py:44
  82.3 31.9 %all-gather.17.cloned.1.call-done = bf16[512,2048]{0,1:T(8,128)(2,1)} async-done(((bf16[128,2048]{0,1:T(8,128)(2,1)}), bf16[512,2048]{0,1:T(8,128)(2,1)}) %all-gather.17.cloned.1.call-update) | async-done | bytes 2097168 | tf_op jit(solution)/shard_map/all_gather | solution.py:44
  119.4 37.1 %all-gather.21.cloned.1.call-done = bf16[4096,256]{1,0:T(8,128)(2,1)} async-done(((bf16[256,256]{1,0:T(8,128)(2,1)}), bf16[4096,256]{1,0:T(8,128)(2,1)}) %all-gather.21.cloned.1.call-update) | async-done | bytes 2097168 | tf_op jit(solution)/shard_map/all_gather | solution.py:44
  184.7 18.8 %all-gather.23.cloned.1.call-done = bf16[512,2048]{0,1:T(8,128)(2,1)} async-done(((bf16[128,2048]{0,1:T(8,128)(2,1)}), bf16[512,2048]{0,1:T(8,128)(2,1)}) %all-gather.23.cloned.1.call-update) | async-done | bytes 2097168 | tf_op jit(solution)/shard_map/all_gather | solution.py:44
  210.0 17.2 %all_to_all.201 = bf16[4,256,512]{2,1,0:T(8,128)(2,1)S(1)} all-to-all(bf16[4,256,512]{2,1,0:T(8,128)(2,1)S(1)} %bitcast.407), channel_id=1, replica_groups=mesh['dp'=2,'row'=4,'col'=4] {'col'}, dimensions={0} | all-to-all | bytes 2097152 | tf_op jit(solution)/shard_map/all_to_all | solution.py:36
  229.1 28.4 %all_to_all.202 = bf16[4,256,512]{2,1,0:T(8,128)(2,1)S(1)} all-to-all(bf16[4,256,512]{2,1,0:T(8,128)(2,1)S(1)} %fusion.58), channel_id=1, replica_groups=mesh['dp'=2,'row'=4,'col'=4] {'col'}, dimensions={0} | all-to-all | bytes 2097152 | tf_op jit(solution)/shard_map/all_to_all | solution.py:36
  284.8 62.0 %all-gather.29.cloned.1.call-done = bf16[1024,2048]{0,1:T(8,128)(2,1)} async-done(((bf16[256,2048]{0,1:T(8,128)(2,1)}), bf16[1024,2048]{0,1:T(8,128)(2,1)}) %all-gather.29.cloned.1.call-update) | async-done | bytes 4194320 | tf_op jit(solution)/shard_map/all_gather | solution.py:44
  346.8 55.2 %all-gather.31.cloned.1.call-done = bf16[2048,2048]{1,0:T(8,128)(2,1)} async-done(((bf16[256,2048]{1,0:T(8,128)(2,1)}), bf16[2048,2048]{1,0:T(8,128)(2,1)}) %all-gather.31.cloned.1.call-update) | async-done | bytes 8388624 | tf_op jit(solution)/shard_map/all_gather | solution.py:44
  416.4 67.8 %all-gather.27.cloned.1.call-done = bf16[1024,2048]{0,1:T(8,128)(2,1)} async-done(((bf16[256,2048]{0,1:T(8,128)(2,1)}), bf16[1024,2048]{0,1:T(8,128)(2,1)}) %all-gather.27.cloned.1.call-update) | async-done | bytes 4194320 | tf_op jit(solution)/shard_map/all_gather | solution.py:44
  484.2 55.1 %all-gather.25.cloned.1.call-done = bf16[2048,2048]{1,0:T(8,128)(2,1)} async-done(((bf16[256,2048]{1,0:T(8,128)(2,1)}), bf16[2048,2048]{1,0:T(8,128)(2,1)}) %all-gather.25.cloned.1.call-update) | async-done | bytes 8388624 | tf_op jit(solution)/shard_map/all_gather | solution.py:44
  539.3 22.2 %fusion.6 = (bf16[2048,1024]{1,0:T(8,128)(2,1)S(1)}, f32[2048,1024]{1,0:T(8,128)}) fusion(f32[2048,1024]{1,0:T(8,128)} %fusion.125, bf16[2048,2048]{1,0:T(8,128)(2,1)} %all-gather.25.cloned.1.call-done, bf16[1024,2048]{0,1:T(8,128)(2,1)} %all-gather.27.cloned.1.call-done), kind=kOutput, calls=%fused_computation.11 | convolution fusion | flops 8631877632 | bytes 33554432 | tf_op jit(solution)/shard_map/dot_general | solution.py:13
  590.0 55.9 %reduce-scatter.15.cloned.1.call-done = bf16[256,2048]{1,0:T(8,128)(2,1)} async-done(((bf16[2048,2048]{1,0:T(8,128)(2,1)}), bf16[256,2048]{1,0:T(8,128)(2,1)}) %reduce-scatter.15.cloned.1.call-update) | async-done | bytes 1048592 | tf_op jit(solution)/shard_map/reduce_scatter | solution.py:48
  648.7 71.8 %reduce-scatter.13.cloned.1.call-done = bf16[256,2048]{1,0:T(8,128)(2,1)} async-done(((bf16[2048,2048]{1,0:T(8,128)(2,1)}), bf16[256,2048]{1,0:T(8,128)(2,1)}) %reduce-scatter.13.cloned.1.call-update) | async-done | bytes 1048592 | tf_op jit(solution)/shard_map/reduce_scatter | solution.py:48
  725.9 34.5 %all-gather.33.cloned.1.call-done = bf16[1024,2048]{1,0:T(8,128)(2,1)} async-done(((bf16[256,2048]{1,0:T(8,128)(2,1)}), bf16[1024,2048]{1,0:T(8,128)(2,1)}) %all-gather.33.cloned.1.call-update) | async-done | bytes 4194320 | tf_op jit(solution)/shard_map/all_gather | solution.py:44
  913.4 75.8 %reduce-scatter.29.cloned.1.call-done = bf16[256,2048]{1,0:T(8,128)(2,1)} async-done(((bf16[1024,2048]{1,0:T(8,128)(2,1)}), bf16[256,2048]{1,0:T(8,128)(2,1)}) %reduce-scatter.29.cloned.1.call-update) | async-done | bytes 1048592 | tf_op jit(solution)/shard_map/reduce_scatter | solution.py:48
  990.5 17.6 %all_to_all.204 = bf16[256,4,512]{2,0,1:T(8,128)(2,1)} all-to-all(bf16[256,4,512]{2,0,1:T(8,128)(2,1)S(1)} %bitcast.416), channel_id=1, replica_groups=mesh['dp'=2,'row'=4,'col'=4] {'col'}, dimensions={1} | all-to-all | bytes 2097152 | tf_op jit(solution)/shard_map/all_to_all | solution.py:40
  1014.3 54.5 %reduce-scatter.27.cloned.1.call-done = bf16[256,2048]{1,0:T(8,128)(2,1)} async-done(((bf16[1024,2048]{1,0:T(8,128)(2,1)}), bf16[256,2048]{1,0:T(8,128)(2,1)}) %reduce-scatter.27.cloned.1.call-update) | async-done | bytes 1048592 | tf_op jit(solution)/shard_map/reduce_scatter | solution.py:48
  1088.5 26.9 %reduce-scatter.21.cloned.1.call-done = bf16[128,2048]{1,0:T(8,128)(2,1)} async-done(((bf16[512,2048]{1,0:T(8,128)(2,1)}), bf16[128,2048]{1,0:T(8,128)(2,1)}) %reduce-scatter.21.cloned.1.call-update) | async-done | bytes 524304 | tf_op jit(solution)/shard_map/reduce_scatter | solution.py:48
  1120.7 40.1 %reduce-scatter.25.cloned.1.call-done = bf16[128,2048]{1,0:T(8,128)(2,1)} async-done(((bf16[512,2048]{1,0:T(8,128)(2,1)}), bf16[128,2048]{1,0:T(8,128)(2,1)}) %reduce-scatter.25.cloned.1.call-update) | async-done | bytes 524304 | tf_op jit(solution)/shard_map/reduce_scatter | solution.py:48
  1189.6 33.1 %all-gather.37.cloned.1.call-done = bf16[2048,512]{1,0:T(8,128)(2,1)} async-done(((bf16[1024,512]{1,0:T(8,128)(2,1)}), bf16[2048,512]{1,0:T(8,128)(2,1)}) %all-gather.37.cloned.1.call-update) | async-done | bytes 2097168 | tf_op jit(solution)/shard_map/all_gather | solution.py:44
  1231.5 39.1 %reduce-scatter.17.cloned.1.call-done = bf16[256,2048]{1,0:T(8,128)(2,1)} async-done(((bf16[1024,2048]{1,0:T(8,128)(2,1)}), bf16[256,2048]{1,0:T(8,128)(2,1)}) %reduce-scatter.17.cloned.1.call-update) | async-done | bytes 1048592 | tf_op jit(solution)/shard_map/reduce_scatter | solution.py:48
  1281.1 24.8 %all-gather.35.cloned.1.call-done = bf16[2048,512]{0,1:T(8,128)(2,1)} async-done(((bf16[1024,512]{0,1:T(8,128)(2,1)}), bf16[2048,512]{0,1:T(8,128)(2,1)}) %all-gather.35.cloned.1.call-update) | async-done | bytes 2097168 | tf_op jit(solution)/shard_map/all_gather | solution.py:44
  1310.0 39.1 %all-reduce.3.cloned.1.call-done = (bf16[512,512]{1,0:T(8,128)(2,1)}, bf16[512,512]{1,0:T(8,128)(2,1)}) async-done(((bf16[512,512]{1,0:T(8,128)(2,1)}, bf16[512,512]{1,0:T(8,128)(2,1)}), (bf16[512,512]{1,0:T(8,128)(2,1)}, bf16[512,512]{1,0:T(8,128)(2,1)})) %all-reduce.3.cloned.1.call-update) | async-done | bytes 1048592 | tf_op jit(solution)/shard_map/psum | solution.py:189
  1353.6 40.6 %psum.21 = f32[4,2048]{1,0:T(4,128)S(1)} all-reduce(f32[4,2048]{1,0:T(4,128)S(1)} %pad_maximum_fusion.2), channel_id=1, replica_groups=mesh['dp'=2,'row'=4,'col'=4] {'dp','row','col'}, use_global_device_ids=true, to_apply=%region_41.42 | all-reduce | flops 8192 | bytes 65536 | tf_op jit(solution)/shard_map/psum | solution.py:187
  (345 shorter events, 431.1 us)
Async XLA Ops:
  8.0 57.8 %all-gather.19.cloned.1.call-start = ((), (), s32[]{:S(2)}) async-start(), calls=%async_computation.23 | async-start | bytes 1310720 | tf_op jit(solution)/shard_map/all_gather | solution.py:44
  8.7 105.5 %all-gather.17.cloned.1.call-start = ((), (), s32[]{:S(2)}) async-start(), calls=%async_computation.22 | async-start | bytes 2621440 | tf_op jit(solution)/shard_map/all_gather | solution.py:44
  24.0 132.5 %all-gather.21.cloned.1.call-start = ((), (), s32[]{:S(2)}) async-start(), calls=%async_computation.24 | async-start | bytes 2228224 | tf_op jit(solution)/shard_map/all_gather | solution.py:44
  71.9 131.5 %all-gather.23.cloned.1.call-start = ((), (), s32[]{:S(2)}) async-start(), calls=%async_computation.25 | async-start | bytes 2621440 | tf_op jit(solution)/shard_map/all_gather | solution.py:44
  81.8 197.1 %reduce-scatter.11.cloned.1.call-start = ((), (), s32[]{:S(2)}) async-start(), calls=%async_computation.26 | async-start | bytes 5242880 | tf_op jit(solution)/shard_map/reduce_scatter | solution.py:48
  209.8 136.9 %all-gather.29.cloned.1.call-start = ((), (), s32[]{:S(2)}) async-start(), calls=%async_computation.29 | async-start | bytes 5242880 | tf_op jit(solution)/shard_map/all_gather | solution.py:44
  228.5 173.5 %all-gather.31.cloned.1.call-start = ((), (), s32[]{:S(2)}) async-start(), calls=%async_computation.31 | async-start | bytes 9437184 | tf_op jit(solution)/shard_map/all_gather | solution.py:44
  258.7 225.6 %all-gather.27.cloned.1.call-start = ((), (), s32[]{:S(2)}) async-start(), calls=%async_computation.28 | async-start | bytes 5242880 | tf_op jit(solution)/shard_map/all_gather | solution.py:44
  278.8 260.5 %all-gather.25.cloned.1.call-start = ((), (), s32[]{:S(2)}) async-start(), calls=%async_computation.27 | async-start | bytes 9437184 | tf_op jit(solution)/shard_map/all_gather | solution.py:44
  284.7 361.2 %reduce-scatter.15.cloned.1.call-start = ((), (), s32[]{:S(2)}) async-start(), calls=%async_computation.32 | async-start | bytes 9437184 | tf_op jit(solution)/shard_map/reduce_scatter | solution.py:48
  574.5 146.1 %reduce-scatter.13.cloned.1.call-start = ((), (), s32[]{:S(2)}) async-start(), calls=%async_computation.30 | async-start | bytes 9437184 | tf_op jit(solution)/shard_map/reduce_scatter | solution.py:48
  589.9 170.5 %all-gather.33.cloned.1.call-start = ((), (), s32[]{:S(2)}) async-start(), calls=%async_computation.33 | async-start | bytes 5242880 | tf_op jit(solution)/shard_map/all_gather | solution.py:44
  725.8 184.9 %reduce-scatter.19.cloned.1.call-start = ((), (), s32[]{:S(2)}) async-start(), calls=%async_computation.35 | async-start | bytes 2228224 | tf_op jit(solution)/shard_map/reduce_scatter | solution.py:48
  849.0 140.3 %reduce-scatter.29.cloned.1.call-start = ((), (), s32[]{:S(2)}) async-start(), calls=%async_computation.41 | async-start | bytes 5242880 | tf_op jit(solution)/shard_map/reduce_scatter | solution.py:48
  865.0 203.8 %reduce-scatter.27.cloned.1.call-start = ((), (), s32[]{:S(2)}) async-start(), calls=%async_computation.39 | async-start | bytes 5242880 | tf_op jit(solution)/shard_map/reduce_scatter | solution.py:48
  879.6 235.8 %reduce-scatter.21.cloned.1.call-start = ((), (), s32[]{:S(2)}) async-start(), calls=%async_computation.36 | async-start | bytes 2621440 | tf_op jit(solution)/shard_map/reduce_scatter | solution.py:48
  898.1 262.7 %reduce-scatter.25.cloned.1.call-start = ((), (), s32[]{:S(2)}) async-start(), calls=%async_computation.38 | async-start | bytes 2621440 | tf_op jit(solution)/shard_map/reduce_scatter | solution.py:48
  904.3 283.8 %reduce-scatter.23.cloned.1.call-start = ((), (), s32[]{:S(2)}) async-start(), calls=%async_computation.37 | async-start | bytes 1310720 | tf_op jit(solution)/shard_map/reduce_scatter | solution.py:48
  913.4 309.3 %all-gather.37.cloned.1.call-start = ((), (), s32[]{:S(2)}) async-start(), calls=%async_computation.42 | async-start | bytes 3145728 | tf_op jit(solution)/shard_map/all_gather | solution.py:44
  1008.2 262.5 %reduce-scatter.17.cloned.1.call-start = ((), (), s32[]{:S(2)}) async-start(), calls=%async_computation.34 | async-start | bytes 5242880 | tf_op jit(solution)/shard_map/reduce_scatter | solution.py:48
  1014.2 291.7 %all-gather.35.cloned.1.call-start = ((), (), s32[]{:S(2)}) async-start(), calls=%async_computation.40 | async-start | bytes 3145728 | tf_op jit(solution)/shard_map/all_gather | solution.py:44
  1166.1 182.9 %all-reduce.3.cloned.1.call-start = ((), (), s32[]{:S(2)}) async-start(), calls=%async_computation.44 | async-start | bytes 2097152 | tf_op jit(solution)/shard_map/psum | solution.py:189
  1175.8 225.0 %all-gather.39.cloned.1.call-start = ((), (), s32[]{:S(2)}) async-start(), calls=%async_computation.43 | async-start | bytes 2359296 | tf_op jit(solution)/shard_map/all_gather | solution.py:9
  1276.8 126.8 %all-to-all-start.6 = ((bf16[256,4,512]{2,0,1:T(8,128)(2,1)}), bf16[256,4,512]{2,0,1:T(8,128)(2,1)}, u32[]{:S(2)}, u32[]{:S(2)}) async-start(bf16[256,4,512]{2,0,1:T(8,128)(2,1)} %bitcast.352), calls=%async_computation.11 | async-start | bytes 2097152 | tf_op jit(solution)/shard_map/all_to_all | solution.py:40
  (65 other events, 1344.2 us)
Sparse Core Ops, SparseCore 0:
  9.6 37.4 all-gather.14
  48.7 17.0 all-gather.18
  67.9 46.2 all-gather.16
  116.8 39.6 all-gather.20
  158.4 44.9 all-gather.22
  209.9 53.9 reduce-scatter.10
  266.2 80.5 all-gather.28
  349.4 52.5 all-gather.30
  403.6 80.5 all-gather.26
  486.7 52.5 all-gather.24
  574.6 71.3 reduce-scatter.14
  649.2 71.2 reduce-scatter.12
  725.9 34.4 all-gather.32
  849.1 61.5 reduce-scatter.18
  913.4 75.7 reduce-scatter.28
  991.5 77.2 reduce-scatter.26
  1070.9 44.3 reduce-scatter.20
  1117.6 43.1 reduce-scatter.24
  1163.9 24.1 reduce-scatter.22
  1189.6 33.1 all-gather.36
  1226.0 44.5 reduce-scatter.16
  1272.7 33.0 all-gather.34
  1308.8 40.2 all-reduce.2
  1351.3 49.5 all-gather.38
